TPU v7x, 32 devices: a whole 2x2x4 slice. The times are simulated.
32 devices in a mesh: rows: 16 (over z, x, core), cols: 2 (over y).
Axes of the slice: x: 2, y: 2, z: 4, core: 2. Of those that a mesh axis runs over, the one named last changes fastest.
Arguments:
- slab: float32 [131072, 512], P('rows', 'cols')
- sign_bits: int32 [131072], P('rows'), may hold values from 0 to 1
- block_mask: int32 [1024], P('rows'), may hold values 0 or 1
- sample_rows: int32 [2048], P('rows'), may hold values from 0 to 8191, as said below
Outputs:
- sketch_rows: float32 [2048, 512], P('rows', 'cols')
- r_factor: float32 [512, 512], P(None, 'cols')
Inputs may be any that keep to these rules, and one draw needn't show every extreme that they name: `sample_rows`: each block of 128 entries names rows of the matching index of rows, as numbers below 8192; rows may repeat.
All inputs are finite; a program needn't handle non-finite values. No bound on the sum of `block_mask` on one device may be relied on, other than what follows from the above.
Results may differ from a plain program's by a relative error of at most 0.00016.
Values sent between devices are 32-bit elements; how exact they have to be, the bound alone decides.
No kernel may reach another device: no remote copies, remote signals or barrier semaphores. Data moves between devices by JAX's collectives and lax.ppermute only.
A program may use at most 64 MiB of HBM per device.

v0:
```python
import math
import jax
import jax.numpy as jnp
from jax import lax
from jax.sharding import PartitionSpec as P


def swapped(value, axis, bit):
    return lax.ppermute(value, axis, [(i, i ^ 1 << bit) for i in range(lax.axis_size(axis))])


def bit_parity(values, bit_total):
    total = jnp.zeros(values.shape, jnp.int32)
    for position in range(bit_total):
        total = total + jnp.bitwise_and(jnp.right_shift(values, position), 1)
    return jnp.bitwise_and(total, 1)


def sylvester(order_size):
    counter = jnp.arange(order_size, dtype=jnp.int32)
    common = jnp.bitwise_and(counter[:, None], counter[None, :])
    parity = bit_parity(common, max(order_size.bit_length(), 1))
    return (1 - 2 * parity).astype(jnp.float32)


def local_mix(scaled):
    block_count = scaled.shape[0]
    block_rows = scaled.shape[1]
    first_pass = jnp.einsum(
        "jb,rbc->rjc", sylvester(block_rows), scaled, precision=lax.Precision.HIGHEST
    )
    return jnp.einsum(
        "ir,rjc->ijc", sylvester(block_count), first_pass, precision=lax.Precision.HIGHEST
    )


def body(slab, sign_bits, block_mask, sample_rows):
    row_count, panel_width = slab.shape
    groups = lax.axis_size("rows")
    block_count = block_mask.shape[0]
    block_rows = row_count // block_count
    norm_scale = 1.0 / math.sqrt(row_count * groups)
    sign_values = (2 * sign_bits - 1).astype(jnp.float32)
    mask_values = block_mask.astype(jnp.float32)
    scaled = slab.reshape(block_count, block_rows, panel_width) * sign_values.reshape(
        block_count, block_rows, 1
    )
    scaled = scaled * mask_values.reshape(block_count, 1, 1)
    mixed_rows = local_mix(scaled).reshape(row_count, panel_width)
    pick_count = sample_rows.shape[0]
    device = lax.axis_index("rows")
    for bit_level in range(groups.bit_length() - 1):
        partner = swapped(mixed_rows, "rows", bit_level)
        high_bit = jnp.bitwise_and(jnp.right_shift(device, bit_level), 1)
        mixed_rows = jnp.where(high_bit == 0, mixed_rows + partner, partner - mixed_rows)
    sketch = jnp.take(mixed_rows, sample_rows, axis=0) * norm_scale
    full_rows = lax.all_gather(sketch, "cols", axis=1, tiled=True)
    panel_index = lax.axis_index("cols")
    local_gram = jnp.einsum("sa,sb->ab", full_rows, full_rows, precision=lax.Precision.HIGHEST)
    gram_matrix = lax.psum(local_gram, "rows")
    gram_matrix = gram_matrix / (pick_count * groups)
    lower_factor = jnp.linalg.cholesky(gram_matrix)
    upper_factor = lower_factor.T
    r_panel = lax.dynamic_slice_in_dim(upper_factor, panel_index * panel_width, panel_width, 1)
    return (sketch, r_panel)


def solution(mesh):
    in_specs = (P("rows", "cols"), P("rows"), P("rows"), P("rows"))
    out_specs = (P("rows", "cols"), P(None, "cols"))
    return jax.shard_map(body, mesh=mesh, in_specs=in_specs, out_specs=out_specs, check_vma=False)
```

profile of v0, /device:TPU:0, one launch (start us, length us, event | category | flops | bytes accessed | tf_op | source)
XLA Modules:
  0.0 1038.9 jit_solution(15961802083530760773)
XLA Ops:
  7.2 0.0 all-reduce.3.cloned.1.call-start
  7.2 0.8 convert_bitcast_fusion
  8.0 0.7 convert_element_type.14
  8.6 19.1 %fusion.2 = f32[64,256,128]{2,1,0:T(8,128)} fusion(f32[64,128,256]{2,1,0:T(8,128)} %bitcast.40, f32[64]{0:T(128)S(1)} %convert_element_type.14, f32[64,128]{1,0:T(8,128)S(1)} %convert_bitcast_fusion), kind=kOutput, calls=%fused_computation.7 | convolution fusion | flops 3225878528 | bytes 16810240 | tf_op jit(solution)/shard_map/jb,rbc->rjc/dot_general | solution.py:29
  27.8 9.2 copy.13
  36.9 10.5 %fusion = f32[64,128,256]{2,0,1:T(8,128)S(1)} fusion(f32[64,256,128]{1,0,2:T(8,128)} %copy.13), kind=kOutput, calls=%fused_computation.1 | convolution fusion | flops 1610715136 | bytes 16777216 | tf_op jit(solution)/shard_map/ir,rjc->ijc/dot_general | solution.py:32
  47.5 8.1 copy.9
  55.5 0.5 collective-permute-start
  56.0 13.1 %collective-permute-done = f32[8192,256]{1,0:T(8,128)} collective-permute-done((f32[8192,256]{1,0:T(8,128)}, f32[8192,256]{1,0:T(8,128)}, u32[]{:S(2)}, u32[]{:S(2)}) %collective-permute-start) | collective-permute-done | bytes 8388640 | tf_op jit(solution)/shard_map/ppermute | solution.py:9
  69.1 10.1 subtract_select_fusion.3
  79.2 2.9 collective-permute-start.1
  82.0 181.1 %collective-permute-done.1 = f32[8192,256]{1,0:T(8,128)} collective-permute-done((f32[8192,256]{1,0:T(8,128)}, f32[8192,256]{1,0:T(8,128)}, u32[]{:S(2)}, u32[]{:S(2)}) %collective-permute-start.1) | collective-permute-done | bytes 8388640 | tf_op jit(solution)/shard_map/ppermute | solution.py:9
  263.1 10.1 subtract_select_fusion.2
  273.2 1.8 collective-permute-start.2
  275.0 0.0 copy-start.1
  275.0 180.5 %collective-permute-done.2 = f32[8192,256]{1,0:T(8,128)} collective-permute-done((f32[8192,256]{1,0:T(8,128)}, f32[8192,256]{1,0:T(8,128)}, u32[]{:S(2)}, u32[]{:S(2)}) %collective-permute-start.2) | collective-permute-done | bytes 8388640 | tf_op jit(solution)/shard_map/ppermute | solution.py:9
  455.5 10.1 subtract_select_fusion.1
  465.5 2.5 collective-permute-start.3
  468.1 0.0 copy-done.1
  468.1 359.5 %collective-permute-done.3 = f32[8192,256]{1,0:T(8,128)} collective-permute-done((f32[8192,256]{1,0:T(8,128)}, f32[8192,256]{1,0:T(8,128)}, u32[]{:S(2)}, u32[]{:S(2)}) %collective-permute-start.3) | collective-permute-done | bytes 8388640 | tf_op jit(solution)/shard_map/ppermute | solution.py:9
  827.6 10.1 subtract_select_fusion
  837.7 4.1 gather_fusion
  841.8 0.1 select_multiply_fusion
  841.9 0.0 copy-start
  841.9 5.8 all_gather.3
  847.7 2.1 fusion.110
  849.8 0.0 all-reduce.3.cloned.1.call-update
  849.8 94.5 %all-reduce.3.cloned.1.call-done = f32[512,512]{0,1:T(8,128)} async-done(((f32[512,512]{0,1:T(8,128)}), f32[512,512]{0,1:T(8,128)}) %all-reduce.3.cloned.1.call-update) | async-done | bytes 1048592 | tf_op jit(solution)/shard_map/psum | solution.py:60
  944.3 1.3 broadcast_multiply_fusion
  945.6 0.3 copy.11
  946.0 1.5 fusion.7
  947.5 11.7 %cholesky.104 = f32[128,128]{1,0:T(8,128)S(1)} custom-call(f32[128,128]{1,0:T(8,128)S(1)} %cholesky.266), custom_call_target="Cholesky" | custom-call | tf_op jit(solution)/shard_map/jit(cholesky)/cholesky | solution.py:62
  959.2 0.1 cholesky.224
  959.3 9.8 custom-call.27
  969.2 0.3 constant_dynamic-update-slice_fusion.1
  969.5 0.3 convolution_subtract_fusion
  969.8 11.9 %cholesky.217 = f32[128,128]{1,0:T(8,128)S(1)} custom-call(f32[128,128]{1,0:T(8,128)S(1)} %cholesky.270), custom_call_target="Cholesky" | custom-call | tf_op jit(solution)/shard_map/jit(cholesky)/cholesky | solution.py:62
  981.8 9.8 custom-call.28
  991.6 0.3 convolution_dynamic-update-slice_fusion
  991.9 0.4 convolution_subtract_fusion.1
  992.3 11.7 %cholesky.238 = f32[128,128]{1,0:T(8,128)S(1)} custom-call(f32[128,128]{1,0:T(8,128)S(1)} %cholesky.275), custom_call_target="Cholesky" | custom-call | tf_op jit(solution)/shard_map/jit(cholesky)/cholesky | solution.py:62
  1004.0 0.7 compare_reduce_fusion.1
  1004.7 9.8 custom-call.29
  1014.6 0.2 convolution_dynamic-update-slice_fusion.1
  1014.8 0.4 convolution_subtract_fusion.2
  1015.2 11.7 %cholesky.255 = f32[128,128]{1,0:T(8,128)S(1)} custom-call(f32[128,128]{1,0:T(8,128)S(1)} %convolution_subtract_fusion.2), custom_call_target="Cholesky" | custom-call | tf_op jit(solution)/shard_map/jit(cholesky)/cholesky | solution.py:62
  1026.9 0.6 compare_reduce_fusion
  1027.5 0.7 compare_reduce_fusion.2
  1030.7 0.1 fusion.9
  1030.8 1.0 copy.12
  1031.8 0.0 copy-done
  (10 shorter events, 0.2 us)
Async XLA Ops:
  7.2 937.2 %all-reduce.3.cloned.1.call-start = ((), (), s32[]{:S(2)}) async-start(), calls=%async_computation | async-start | bytes 2097152 | tf_op jit(solution)/shard_map/psum | solution.py:60
  55.5 13.6 %collective-permute-start = (f32[8192,256]{1,0:T(8,128)}, f32[8192,256]{1,0:T(8,128)}, u32[]{:S(2)}, u32[]{:S(2)}) collective-permute-start(f32[8192,256]{1,0:T(8,128)} %bitcast.5), channel_id=1, source_target_pairs={{0,2},{2,0},{4,6},{6,4},{8,10},{10,8},{12,14},{14,12},{16,18},{18,... | collective-permute-start | bytes 25165832 | tf_op jit(solution)/shard_map/ppermute | solution.py:9
  79.2 183.9 %collective-permute-start.1 = (f32[8192,256]{1,0:T(8,128)}, f32[8192,256]{1,0:T(8,128)}, u32[]{:S(2)}, u32[]{:S(2)}) collective-permute-start(f32[8192,256]{1,0:T(8,128)} %subtract_select_fusion.3), channel_id=1, source_target_pairs={{0,4},{2,6},{4,0},{6,2},{8,12},{10,14},{12,8},{14,10},{16,20},{18,... | collective-permute-start | bytes 25165832 | tf_op jit(solution)/shard_map/ppermute | solution.py:9
  273.2 182.3 %collective-permute-start.2 = (f32[8192,256]{1,0:T(8,128)}, f32[8192,256]{1,0:T(8,128)}, u32[]{:S(2)}, u32[]{:S(2)}) collective-permute-start(f32[8192,256]{1,0:T(8,128)} %subtract_select_fusion.2), channel_id=1, source_target_pairs={{0,8},{2,10},{4,12},{6,14},{8,0},{10,2},{12,4},{14,6},{16,24},{18,... | collective-permute-start | bytes 25165832 | tf_op jit(solution)/shard_map/ppermute | solution.py:9
  275.0 193.1 %copy-start.1 = (s32[128]{0:T(128)S(1)}, s32[128]{0:T(128)}, u32[]{:S(2)}) copy-start(s32[128]{0:T(128)} %param.7) | copy-start | bytes 1540
  465.5 362.1 %collective-permute-start.3 = (f32[8192,256]{1,0:T(8,128)}, f32[8192,256]{1,0:T(8,128)}, u32[]{:S(2)}, u32[]{:S(2)}) collective-permute-start(f32[8192,256]{1,0:T(8,128)} %subtract_select_fusion.1), channel_id=1, source_target_pairs={{0,16},{2,18},{4,20},{6,22},{8,24},{10,26},{12,28},{14,30},{16,0},... | collective-permute-start | bytes 25165832 | tf_op jit(solution)/shard_map/ppermute | solution.py:9
  841.9 189.9 %copy-start = (f32[128,256]{1,0:T(8,128)}, f32[128,256]{1,0:T(8,128)S(1)}, u32[]{:S(2)}) copy-start(f32[128,256]{1,0:T(8,128)S(1)} %select_multiply_fusion) | copy-start | bytes 393220
Sparse Core Ops, SparseCore 0:
  849.9 94.3 all-reduce.2
where the time goes:
time: 1050 us; the launch traced here: 1040 us
  waiting for transfers between devices  829 us (79%)
  other arithmetic  123 us (12%)
  matrix products  33.6 us (3%)
  local copies, waits for them, and re-layouts  22.9 us (2%)
  between operations  17 us (2%)
    ppermute x4, waiting for transfers between devices, swapped(): lax.ppermute(value, axis, [(i, i ^ 1 << bit) for i in range(lax.axis_size...  734 us
    psum x1, waiting for transfers between devices, body(): gram_matrix = lax.psum(local_gram, 'rows')  94.5 us
    another operation x14, other arithmetic, body(): lower_factor = jnp.linalg.cholesky(gram_matrix)  78.6 us
    select_n x4, other arithmetic, body(): jnp.where(high_bit == 0, mixed_rows + partner, partner - mixed_rows)  40.3 us
  transfers between devices with their start and end apart: 5, of which 5 were waited for; matrix products, arithmetic and copies ran while one was open for 0% of the time, Pallas kernels for 0%

commit v1 on v0

--- a/solution.py
+++ b/solution.py
@@ -57,7 +57,8 @@
     full_rows = lax.all_gather(sketch, "cols", axis=1, tiled=True)
     panel_index = lax.axis_index("cols")
     local_gram = jnp.einsum("sa,sb->ab", full_rows, full_rows, precision=lax.Precision.HIGHEST)
-    gram_matrix = lax.psum(local_gram, "rows")
+    blocks = lax.all_gather(local_gram, "rows")
+    gram_matrix = jnp.sum(blocks, axis=0)
     gram_matrix = gram_matrix / (pick_count * groups)
     lower_factor = jnp.linalg.cholesky(gram_matrix)
     upper_factor = lower_factor.T

time: 1050 us -> 1080 us (1.029)
  waiting for transfers between devices: 829 us -> 862 us
    all_gather x0 -> x1, waiting for transfers between devices: none -> 128 us  [body(): blocks = lax.all_gather(local_gram, 'rows')]
    psum x1 -> x0, waiting for transfers between devices: 94.5 us -> none  [body(): gram_matrix = lax.psum(local_gram, 'rows')]
where the time goes in v1:
time: 1080 us
  waiting for transfers between devices  862 us (80%)
  other arithmetic  127 us (12%)
  local copies, waits for them, and re-layouts  31.9 us (3%)
  matrix products  25.4 us (2%)
  between operations  17 us (2%)
    ppermute x4, waiting for transfers between devices, swapped(): lax.ppermute(value, axis, [(i, i ^ 1 << bit) for i in range(lax.axis_size...  734 us
    all_gather x1, waiting for transfers between devices, body(): blocks = lax.all_gather(local_gram, 'rows')  128 us
    another operation x14, other arithmetic, body(): lower_factor = jnp.linalg.cholesky(gram_matrix)  78.9 us
    select_n x4, other arithmetic, body(): jnp.where(high_bit == 0, mixed_rows + partner, partner - mixed_rows)  40.3 us
  transfers between devices with their start and end apart: 5, of which 5 were waited for; matrix products, arithmetic and copies ran while one was open for 0% of the time, Pallas kernels for 0%

profile of v1, /device:TPU:0, one launch (start us, length us, event | category | flops | bytes accessed | tf_op | source)
XLA Modules:
  0.0 1077.7 jit_solution(13816487066855370113)
XLA Ops:
  7.2 0.0 all-gather.3.cloned.1.call-start
  7.2 0.0 copy-start.1
  7.2 0.0 copy-start.2
  7.2 9.0 copy.11
  16.2 0.0 copy-done.1
  16.2 0.0 copy-done.2
  16.3 10.9 %fusion.5 = f32[64,128,256]{1,2,0:T(8,128)} fusion(f32[64,128,256]{1,2,0:T(8,128)} %copy.11, f32[64]{0:T(128)S(1)} %convert_element_type.14, f32[64,128]{1,0:T(8,128)S(1)} %convert_bitcast_fusion), kind=kOutput, calls=%fused_computation.10 | convolution fusion | flops 3225878528 | bytes 16810240 | tf_op jit(solution)/shard_map/jb,rbc->rjc/dot_general | solution.py:29
  27.2 9.2 copy.12
  36.4 10.6 fusion.53
  47.0 8.1 copy.13
  55.0 0.5 collective-permute-start
  55.5 13.1 %collective-permute-done = f32[8192,256]{1,0:T(8,128)} collective-permute-done((f32[8192,256]{1,0:T(8,128)}, f32[8192,256]{1,0:T(8,128)}, u32[]{:S(2)}, u32[]{:S(2)}) %collective-permute-start) | collective-permute-done | bytes 8388640 | tf_op jit(solution)/shard_map/ppermute | solution.py:9
  68.6 10.1 subtract_select_fusion.3
  78.7 2.9 collective-permute-start.1
  81.5 181.1 %collective-permute-done.1 = f32[8192,256]{1,0:T(8,128)} collective-permute-done((f32[8192,256]{1,0:T(8,128)}, f32[8192,256]{1,0:T(8,128)}, u32[]{:S(2)}, u32[]{:S(2)}) %collective-permute-start.1) | collective-permute-done | bytes 8388640 | tf_op jit(solution)/shard_map/ppermute | solution.py:9
  262.6 10.1 subtract_select_fusion.2
  272.7 1.8 collective-permute-start.2
  274.5 0.0 copy-start.3
  274.5 180.5 %collective-permute-done.2 = f32[8192,256]{1,0:T(8,128)} collective-permute-done((f32[8192,256]{1,0:T(8,128)}, f32[8192,256]{1,0:T(8,128)}, u32[]{:S(2)}, u32[]{:S(2)}) %collective-permute-start.2) | collective-permute-done | bytes 8388640 | tf_op jit(solution)/shard_map/ppermute | solution.py:9
  455.0 10.1 subtract_select_fusion.1
  465.0 2.5 collective-permute-start.3
  467.6 0.0 copy-done.3
  467.6 359.5 %collective-permute-done.3 = f32[8192,256]{1,0:T(8,128)} collective-permute-done((f32[8192,256]{1,0:T(8,128)}, f32[8192,256]{1,0:T(8,128)}, u32[]{:S(2)}, u32[]{:S(2)}) %collective-permute-start.3) | collective-permute-done | bytes 8388640 | tf_op jit(solution)/shard_map/ppermute | solution.py:9
  827.1 10.1 subtract_select_fusion
  837.2 4.1 gather_fusion
  841.3 0.1 select_multiply_fusion
  841.4 0.0 copy-start
  841.4 5.8 all_gather.9
  847.2 2.0 fusion.112
  849.3 0.0 all-gather.3.cloned.1.call-update
  849.3 128.2 %all-gather.3.cloned.1.call-done = f32[8192,512]{1,0:T(8,128)} async-done(((f32[512,512]{1,0:T(8,128)}), f32[8192,512]{1,0:T(8,128)}) %all-gather.3.cloned.1.call-update) | async-done | bytes 16777232 | tf_op jit(solution)/shard_map/all_gather | solution.py:60
  977.5 7.9 reduce_sum.11
  985.4 0.0 copy-done
  985.5 0.3 copy.14
  985.8 0.2 fusion.8
  986.0 11.7 %cholesky.104 = f32[128,128]{1,0:T(8,128)S(1)} custom-call(f32[128,128]{1,0:T(8,128)S(1)} %cholesky.266), custom_call_target="Cholesky" | custom-call | tf_op jit(solution)/shard_map/jit(cholesky)/cholesky | solution.py:63
  997.8 0.1 cholesky.224
  997.9 9.8 custom-call.27
  1007.7 0.3 constant_dynamic-update-slice_fusion.1
  1008.1 0.3 convolution_subtract_fusion
  1008.4 11.9 %cholesky.217 = f32[128,128]{1,0:T(8,128)S(1)} custom-call(f32[128,128]{1,0:T(8,128)S(1)} %cholesky.270), custom_call_target="Cholesky" | custom-call | tf_op jit(solution)/shard_map/jit(cholesky)/cholesky | solution.py:63
  1020.4 9.8 custom-call.28
  1030.2 0.3 convolution_dynamic-update-slice_fusion
  1030.4 0.4 convolution_subtract_fusion.1
  1030.8 11.7 %cholesky.238 = f32[128,128]{1,0:T(8,128)S(1)} custom-call(f32[128,128]{1,0:T(8,128)S(1)} %cholesky.275), custom_call_target="Cholesky" | custom-call | tf_op jit(solution)/shard_map/jit(cholesky)/cholesky | solution.py:63
  1042.6 0.7 compare_reduce_fusion.1
  1043.3 9.8 custom-call.29
  1053.1 0.2 convolution_dynamic-update-slice_fusion.1
  1053.3 0.4 convolution_subtract_fusion.2
  1053.7 11.9 %cholesky.255 = f32[128,128]{1,0:T(8,128)S(1)} custom-call(f32[128,128]{1,0:T(8,128)S(1)} %convolution_subtract_fusion.2), custom_call_target="Cholesky" | custom-call | tf_op jit(solution)/shard_map/jit(cholesky)/cholesky | solution.py:63
  1065.7 0.6 compare_reduce_fusion
  1066.3 0.7 compare_reduce_fusion.2
  1069.5 0.1 fusion.10
  1069.6 1.0 copy.15
  (12 shorter events, 0.2 us)
Async XLA Ops:
  7.2 970.4 %all-gather.3.cloned.1.call-start = ((), (), s32[]{:S(2)}) async-start(), calls=%async_computation | async-start | bytes 17825792 | tf_op jit(solution)/shard_map/all_gather | solution.py:60
  7.2 9.0 copy-start.1
  7.2 9.0 copy-start.2
  55.0 13.6 %collective-permute-start = (f32[8192,256]{1,0:T(8,128)}, f32[8192,256]{1,0:T(8,128)}, u32[]{:S(2)}, u32[]{:S(2)}) collective-permute-start(f32[8192,256]{1,0:T(8,128)} %bitcast.5), channel_id=1, source_target_pairs={{0,2},{2,0},{4,6},{6,4},{8,10},{10,8},{12,14},{14,12},{16,18},{18,... | collective-permute-start | bytes 25165832 | tf_op jit(solution)/shard_map/ppermute | solution.py:9
  78.7 183.9 %collective-permute-start.1 = (f32[8192,256]{1,0:T(8,128)}, f32[8192,256]{1,0:T(8,128)}, u32[]{:S(2)}, u32[]{:S(2)}) collective-permute-start(f32[8192,256]{1,0:T(8,128)} %subtract_select_fusion.3), channel_id=1, source_target_pairs={{0,4},{2,6},{4,0},{6,2},{8,12},{10,14},{12,8},{14,10},{16,20},{18,... | collective-permute-start | bytes 25165832 | tf_op jit(solution)/shard_map/ppermute | solution.py:9
  272.7 182.3 %collective-permute-start.2 = (f32[8192,256]{1,0:T(8,128)}, f32[8192,256]{1,0:T(8,128)}, u32[]{:S(2)}, u32[]{:S(2)}) collective-permute-start(f32[8192,256]{1,0:T(8,128)} %subtract_select_fusion.2), channel_id=1, source_target_pairs={{0,8},{2,10},{4,12},{6,14},{8,0},{10,2},{12,4},{14,6},{16,24},{18,... | collective-permute-start | bytes 25165832 | tf_op jit(solution)/shard_map/ppermute | solution.py:9
  274.5 193.1 %copy-start.3 = (s32[128]{0:T(128)S(1)}, s32[128]{0:T(128)}, u32[]{:S(2)}) copy-start(s32[128]{0:T(128)} %param.7) | copy-start | bytes 1540
  465.0 362.1 %collective-permute-start.3 = (f32[8192,256]{1,0:T(8,128)}, f32[8192,256]{1,0:T(8,128)}, u32[]{:S(2)}, u32[]{:S(2)}) collective-permute-start(f32[8192,256]{1,0:T(8,128)} %subtract_select_fusion.1), channel_id=1, source_target_pairs={{0,16},{2,18},{4,20},{6,22},{8,24},{10,26},{12,28},{14,30},{16,0},... | collective-permute-start | bytes 25165832 | tf_op jit(solution)/shard_map/ppermute | solution.py:9
  841.4 144.0 %copy-start = (f32[128,256]{1,0:T(8,128)}, f32[128,256]{1,0:T(8,128)S(1)}, u32[]{:S(2)}) copy-start(f32[128,256]{1,0:T(8,128)S(1)} %select_multiply_fusion) | copy-start | bytes 393220
Sparse Core Ops, SparseCore 0:
  849.4 128.0 all-gather.2
